TPU v7x, 256 devices: a whole 4x4x8 slice. The times are simulated.
256 devices in a mesh: track: 64 (over y, z, core), det: 4 (over x).
Axes of the slice: x: 4, y: 4, z: 8, core: 2. Of those that a mesh axis runs over, the one named last changes fastest.
Arguments:
- jac: float32 [32768, 12, 512], P('track', None, 'det'), may hold values from -1.75 to 1.75
- obs: float32 [32768, 512], P('track', 'det'), may hold values from -6 to 6
- match: int32 [32768], P('track'), may hold values from 0 to 32767, as said below
- tile_knot: int32 [32768], P('track'), may hold values from 0 to 127
- tile_frac: float32 [32768], P('track'), may hold values from 0 to 1
Outputs:
- knot_field: float32 [12, 8192], P(None, 'track')
- tie_residual: float32 [32768, 512], P('track', 'det')
Inputs may be any that keep to these rules, and one draw needn't show every extreme that they name: match[match[i]] = i and match[i] != i; the tiles of each index of track cross exactly 8 tiles of every index of track, itself included.
All inputs are finite; a program needn't handle non-finite values.
Results may differ from a plain program's by a relative error of at most 0.0001.
Values sent between devices are 32-bit elements; how exact they have to be, the bound alone decides.
A program may use at most 64 MiB of HBM per device.

v0:
```python
import jax
import jax.numpy as jnp
from jax import lax
from jax.sharding import PartitionSpec as P

KNOT_DEV = 128
ITERS = 4


damping = 1.0


def passed_along(value, axis, steps):
    count = lax.axis_size(axis)
    leading, last = (max(0, -steps), min(count, count - steps))
    return lax.ppermute(value, axis, [(source, source + steps) for source in range(leading, last)])


def local(jac, obs, match, tile_knot, tile_frac):
    highest = lax.Precision.HIGHEST
    tiles_dev = jac.shape[0]
    params = jac.shape[1]
    n_track = lax.axis_size("track")
    n_det = lax.axis_size("det")
    per_peer = tiles_dev // n_track
    send_order = jnp.argsort(match // tiles_dev, stable=True)

    def arrange(values):
        return values[send_order].reshape((n_track, per_peer) + values.shape[1:])

    slots_in = lax.all_to_all(
        arrange(match % tiles_dev), "track", split_axis=0, concat_axis=0, tiled=True
    )
    receive_order = jnp.argsort(slots_in.reshape(-1))

    def settle(arrived):
        joined = arrived.reshape((tiles_dev,) + arrived.shape[2:])
        return joined[receive_order]

    def partner_values(values):
        return settle(
            lax.all_to_all(arrange(values), "track", split_axis=0, concat_axis=0, tiled=True)
        )

    knot_rows = lax.broadcasted_iota(jnp.int32, (KNOT_DEV, tiles_dev), 0)
    weights = jnp.where(knot_rows == tile_knot[None, :], 1.0 - tile_frac[None, :], 0.0)
    weights = weights + jnp.where(knot_rows == tile_knot[None, :] + 1, tile_frac[None, :], 0.0)
    weights_back = weights.T
    edge_weight = jnp.where(tile_knot == KNOT_DEV - 1, tile_frac, 0.0)
    misfit = obs - partner_values(obs)

    def adjoint(residual_rows):
        partial_value = jnp.einsum("ipw,iw->pi", jac, residual_rows, precision=highest)
        partial_value = lax.psum(partial_value, "det")
        spread = jnp.dot(partial_value, weights_back, precision=highest)
        spill_over = jnp.dot(partial_value, edge_weight, precision=highest)
        carried = passed_along(spill_over, "track", 1)
        return spread.at[:, 0].add(carried)

    def slope_total(gradient):
        return lax.psum(jnp.sum(gradient * gradient), "track")

    knot_field = jnp.zeros((params, KNOT_DEV), jnp.float32)
    tie_residual = misfit
    gradient = adjoint(tie_residual)
    direction = gradient
    slope_norm = slope_total(gradient)
    for iteration in range(ITERS):
        following = passed_along(direction[:, 0], "track", -1)
        interp = (
            jnp.dot(direction, weights, precision=highest)
            + following[:, None] * edge_weight[None, :]
        )
        own_pred = jnp.einsum("ipw,pi->iw", jac, interp, precision=highest)
        other_pred = partner_values(own_pred)
        change = own_pred - other_pred
        change_sq, direction_sq = lax.psum(
            (jnp.sum(change * change), jnp.sum(direction * direction)), ("track", "det")
        )
        curvature = 0.5 * change_sq + damping * direction_sq / n_det
        step_length = slope_norm / curvature
        knot_field = knot_field + step_length * direction
        tie_residual = tie_residual - step_length * change
        gradient = adjoint(tie_residual) - damping * knot_field
        new_norm = slope_total(gradient)
        direction = gradient + new_norm / slope_norm * direction
        slope_norm = new_norm
    return (knot_field, tie_residual)


def solution(mesh):
    in_specs = (P("track", None, "det"), P("track", "det"), P("track"), P("track"), P("track"))
    out_specs = (P(None, "track"), P("track", "det"))
    return jax.shard_map(local, mesh=mesh, in_specs=in_specs, out_specs=out_specs, check_vma=False)
```

profile of v0, /device:TPU:1, one launch (start us, length us, event | category | flops | bytes accessed | tf_op | source)
XLA Modules:
  0.0 1151.6 jit_solution(3248454608757837504)
XLA Ops:
  1.5 3.8 sort.34
  5.3 3.5 gather_fusion.1
  9.5 13.1 %all-to-all-start.1 = ((s32[64,1,8]{2,1,0:T(1,128)}), s32[64,1,8]{2,1,0:T(1,128)S(1)}, u32[]{:S(2)}, u32[]{:S(2)}) async-start(s32[64,1,8]{2,1,0:T(1,128)} %bitcast.2), calls=%async_computation.1 | async-start | bytes 65536 | tf_op jit(solution)/shard_map/all_to_all | solution.py:31
  25.7 6.2 all-to-all-done.1
  32.0 5.5 all-to-all-start
  38.8 3.8 sort.35
  42.6 6.8 all-to-all-done
  49.4 2.6 gather_fusion.2
  53.7 7.9 fusion.14
  61.6 16.6 %psum.112 = f32[12,512]{0,1:T(8,128)} all-reduce(f32[12,512]{0,1:T(8,128)S(1)} %bitcast.110), channel_id=1, replica_groups=mesh['track'=64,'det'=4] {'det'}, use_global_device_ids=true, to_apply=%region_2.3 | all-reduce | flops 6144 | bytes 49152 | tf_op jit(solution)/shard_map/psum | solution.py:54
  79.4 7.5 collective-permute-start
  91.4 3.0 collective-permute-done.1
  95.5 6.3 fusion.12
  103.4 9.0 all-to-all-start.2
  113.1 124.9 %psum.113 = f32[]{:T(128)} all-reduce(f32[]{:T(128)} %multiply_reduce_fusion.10), channel_id=1, replica_groups=mesh['track'=64,'det'=4] {'track'}, use_global_device_ids=true, to_apply=%region_5.6 | all-reduce | flops 1 | bytes 8 | tf_op jit(solution)/shard_map/psum | solution.py:61
  238.1 2.6 gather_fusion.4
  240.7 2.3 multiply_reduce_fusion.3
  242.9 75.7 %all-reduce.3 = (f32[]{:T(128)}, f32[]{:T(128)}) all-reduce(f32[]{:T(128)} %get-tuple-element.77, f32[]{:T(128)} %multiply_reduce_fusion.10), channel_id=1, replica_groups=mesh['track'=64,'det'=4] {'track','det'}, use_global_device_ids=true, to_apply=%region_7.8 | all-reduce | flops 2 | bytes 16 | tf_op jit(solution)/shard_map/psum | solution.py:77
  322.2 7.9 fusion.10
  330.1 16.5 %psum.116 = f32[12,512]{0,1:T(8,128)} all-reduce(f32[12,512]{0,1:T(8,128)S(1)} %bitcast.111), channel_id=1, replica_groups=mesh['track'=64,'det'=4] {'det'}, use_global_device_ids=true, to_apply=%region_9.10 | all-reduce | flops 6144 | bytes 49152 | tf_op jit(solution)/shard_map/psum | solution.py:54
  349.3 8.1 collective-permute-start.2
  359.6 121.8 %psum.117 = f32[]{:T(128)} all-reduce(f32[]{:T(128)} %multiply_reduce_fusion.9), channel_id=1, replica_groups=mesh['track'=64,'det'=4] {'track'}, use_global_device_ids=true, to_apply=%region_11.12 | all-reduce | flops 1 | bytes 8 | tf_op jit(solution)/shard_map/psum | solution.py:61
  483.4 5.6 collective-permute-start.3
  490.6 6.3 fusion.8
  498.6 17.1 %all_to_all.34 = f32[64,8,128]{2,1,0:T(8,128)} all-to-all(f32[64,8,128]{2,1,0:T(8,128)} %bitcast.117), channel_id=1, replica_groups=mesh['track'=64,'det'=4] {'track'}, dimensions={0} | all-to-all | bytes 524288 | tf_op jit(solution)/shard_map/all_to_all | solution.py:42
  515.7 2.6 gather_fusion.6
  518.3 2.4 multiply_reduce_fusion.2
  520.6 74.9 %all-reduce.2 = (f32[]{:T(128)}, f32[]{:T(128)}) all-reduce(f32[]{:T(128)} %get-tuple-element.75, f32[]{:T(128)} %get-tuple-element.73), channel_id=1, replica_groups=mesh['track'=64,'det'=4] {'track','det'}, use_global_device_ids=true, to_apply=%region_13.14 | all-reduce | flops 2 | bytes 16 | tf_op jit(solution)/shard_map/psum | solution.py:77
  599.1 7.9 fusion.6
  607.0 15.1 %psum.120 = f32[12,512]{0,1:T(8,128)} all-reduce(f32[12,512]{0,1:T(8,128)S(1)} %bitcast.112), channel_id=1, replica_groups=mesh['track'=64,'det'=4] {'det'}, use_global_device_ids=true, to_apply=%region_16.17 | all-reduce | flops 6144 | bytes 49152 | tf_op jit(solution)/shard_map/psum | solution.py:54
  624.8 8.4 collective-permute-start.4
  635.4 121.8 %psum.121 = f32[]{:T(128)} all-reduce(f32[]{:T(128)} %get-tuple-element.70), channel_id=1, replica_groups=mesh['track'=64,'det'=4] {'track'}, use_global_device_ids=true, to_apply=%region_18.19 | all-reduce | flops 1 | bytes 8 | tf_op jit(solution)/shard_map/psum | solution.py:61
  759.2 5.4 collective-permute-start.5
  766.4 6.3 fusion.4
  774.4 17.2 %all_to_all.35 = f32[64,8,128]{2,1,0:T(8,128)} all-to-all(f32[64,8,128]{2,1,0:T(8,128)} %bitcast.118), channel_id=1, replica_groups=mesh['track'=64,'det'=4] {'track'}, dimensions={0} | all-to-all | bytes 524288 | tf_op jit(solution)/shard_map/all_to_all | solution.py:42
  791.5 2.6 gather_fusion.8
  794.1 2.3 multiply_reduce_fusion.1
  796.4 74.8 %all-reduce.1 = (f32[]{:T(128)}, f32[]{:T(128)}) all-reduce(f32[]{:T(128)} %get-tuple-element.68, f32[]{:T(128)} %get-tuple-element.66), channel_id=1, replica_groups=mesh['track'=64,'det'=4] {'track','det'}, use_global_device_ids=true, to_apply=%region_20.21 | all-reduce | flops 2 | bytes 16 | tf_op jit(solution)/shard_map/psum | solution.py:77
  874.9 7.9 fusion.2
  882.8 15.2 %psum.124 = f32[12,512]{0,1:T(8,128)} all-reduce(f32[12,512]{0,1:T(8,128)S(1)} %bitcast.113), channel_id=1, replica_groups=mesh['track'=64,'det'=4] {'det'}, use_global_device_ids=true, to_apply=%region_23.24 | all-reduce | flops 6144 | bytes 49152 | tf_op jit(solution)/shard_map/psum | solution.py:54
  900.7 8.5 collective-permute-start.6
  911.4 121.8 %psum.125 = f32[]{:T(128)} all-reduce(f32[]{:T(128)} %multiply_reduce_fusion.5), channel_id=1, replica_groups=mesh['track'=64,'det'=4] {'track'}, use_global_device_ids=true, to_apply=%region_25.26 | all-reduce | flops 1 | bytes 8 | tf_op jit(solution)/shard_map/psum | solution.py:61
  1035.3 5.5 collective-permute-start.7
  1042.5 6.3 fusion
  1050.5 17.2 %all_to_all.36 = f32[64,8,128]{2,1,0:T(8,128)} all-to-all(f32[64,8,128]{2,1,0:T(8,128)} %bitcast.116), channel_id=1, replica_groups=mesh['track'=64,'det'=4] {'track'}, dimensions={0} | all-to-all | bytes 524288 | tf_op jit(solution)/shard_map/all_to_all | solution.py:42
  1067.6 2.6 gather_fusion.10
  1070.2 2.3 multiply_reduce_fusion
  1072.5 74.3 %all-reduce = (f32[]{:T(128)}, f32[]{:T(128)}) all-reduce(f32[]{:T(128)} %get-tuple-element.64, f32[]{:T(128)} %get-tuple-element.62), channel_id=1, replica_groups=mesh['track'=64,'det'=4] {'track','det'}, use_global_device_ids=true, to_apply=%region_27.28 | all-reduce | flops 2 | bytes 16 | tf_op jit(solution)/shard_map/psum | solution.py:77
  (88 shorter events, 51.1 us)
Async XLA Ops:
  0.6 53.1 %copy-start = (f32[512,12,128]{2,0,1:T(8,128)S(1)}, f32[512,12,128]{2,0,1:T(8,128)}, u32[]{:S(2)}) copy-start(f32[512,12,128]{2,0,1:T(8,128)} %param.13) | copy-start | bytes 9437188
  0.6 36.8 %copy-start.6 = (s32[512]{0:T(512)S(1)}, s32[512]{0:T(512)}, u32[]{:S(2)}) copy-start(s32[512]{0:T(512)} %param.16) | copy-start | bytes 6148
  0.7 22.7 %copy-start.1 = (f32[512,128]{1,0:T(8,128)S(1)}, f32[512,128]{1,0:T(8,128)}, u32[]{:S(2)}) copy-start(f32[512,128]{1,0:T(8,128)} %param.14) | copy-start | bytes 786436
  9.5 22.5 %all-to-all-start.1 = ((s32[64,1,8]{2,1,0:T(1,128)}), s32[64,1,8]{2,1,0:T(1,128)S(1)}, u32[]{:S(2)}, u32[]{:S(2)}) async-start(s32[64,1,8]{2,1,0:T(1,128)} %bitcast.2), calls=%async_computation.1 | async-start | bytes 65536 | tf_op jit(solution)/shard_map/all_to_all | solution.py:31
  32.0 17.4 %all-to-all-start = ((f32[64,8,128]{2,1,0:T(8,128)}), f32[64,8,128]{2,1,0:T(8,128)}, u32[]{:S(2)}, u32[]{:S(2)}) async-start(f32[64,8,128]{2,1,0:T(8,128)} %bitcast.114), calls=%async_computation | async-start | bytes 524288 | tf_op jit(solution)/shard_map/all_to_all | solution.py:42
  52.0 34.9 %copy-start.7 = (f32[512]{0:T(512)S(1)}, f32[512]{0:T(512)}, u32[]{:S(2)}) copy-start(f32[512]{0:T(512)} %param.17) | copy-start | bytes 6148
  53.0 0.7 copy-start.2
  79.4 9.0 collective-permute-start
  89.4 4.9 collective-permute-start.1
  103.4 134.6 %all-to-all-start.2 = ((f32[64,8,128]{2,1,0:T(8,128)}), f32[64,8,128]{2,1,0:T(8,128)}, u32[]{:S(2)}, u32[]{:S(2)}) async-start(f32[64,8,128]{2,1,0:T(8,128)} %bitcast.115), calls=%async_computation.2 | async-start | bytes 524288 | tf_op jit(solution)/shard_map/all_to_all | solution.py:42
  321.5 0.7 copy-start.5
  349.3 8.8 collective-permute-start.2
  483.4 6.0 collective-permute-start.3
  598.4 0.7 copy-start.4
  624.8 9.1 collective-permute-start.4
  759.2 6.0 collective-permute-start.5
  874.2 0.7 copy-start.3
  900.7 9.2 collective-permute-start.6
  1035.3 6.0 collective-permute-start.7
where the time goes:
time: 1160 us; the launch traced here: 1150 us
  blocking collectives  905 us (78%)
  starting transfers between devices  78.6 us (7%)
  matrix products  68.8 us (6%)
  other arithmetic  33.7 us (3%)
  local copies, waits for them, and re-layouts  33.2 us (3%)
  waiting for transfers between devices  19.6 us (2%)
  between operations  12.7 us (1%)
    psum x4, blocking collectives, slope_total(): return lax.psum(jnp.sum(gradient * gradient), 'track')  490 us
    psum x4, blocking collectives, local(): lax.psum((jnp.sum(change * change), jnp.sum(direction * direction)), ('tr...  300 us
    psum x4, blocking collectives, adjoint(): partial_value = lax.psum(partial_value, 'det')  63.4 us
    all_to_all x3, blocking collectives, partner_values(): lax.all_to_all(arrange(values), 'track', split_axis=0, concat_axis=0, til...  51.5 us
    ppermute x8, starting transfers between devices, passed_along(): lax.ppermute(value, axis, [(source, source + steps) for source in range(l...  51 us
    dot_general x4, matrix products, adjoint(): jnp.einsum('ipw,iw->pi', jac, residual_rows, precision=highest)  31.6 us
    dot_general x4, matrix products, local(): own_pred = jnp.einsum('ipw,pi->iw', jac, interp, precision=highest)  25.3 us
  transfers between devices with their start and end apart: 11, of which 9 were waited for; matrix products, arithmetic and copies ran while one was open for 1% of the time, Pallas kernels for 0%

commit v1 on v0

v1 whole, which is shorter than its diff:
```python
import functools

import jax
import jax.numpy as jnp
from jax import lax
from jax.experimental import pallas as pl
from jax.experimental.pallas import tpu as pltpu
from jax.sharding import PartitionSpec as P

KNOT_DEV = 128
ITERS = 4
LANES = 128
ROWS = 16
MESH = pl.DeviceIdType.MESH
F32 = jnp.float32
BF16 = jnp.bfloat16

damping = 1.0


def split3(value):
    high = value.astype(BF16)
    rest = value - high.astype(F32)
    mid = rest.astype(BF16)
    low = (rest - mid.astype(F32)).astype(BF16)
    return high, mid, low


def iota(shape, dim):
    return lax.broadcasted_iota(jnp.int32, shape, dim)


def kernel(
    n_track, n_det,
    jac_hbm, obs_ref, match_ref, knot_ref, frac_ref,
    x_out, r_out,
    jac_in, jac_t, sel, sel_t, hot, weight, pred, arrived, fd_ref, r_ref, spread_ref, upd_ref,
    det_send, det_got, prev_got, next_got, gam_send, gam_got, q1_send, q1_got, q2_send, q2_got,
    jac_sem, a_send, a_recv, d_send, d_recv, e_recv, h_recv, g_ssem, g_rsem, q1_ssem, q1_rsem, q2_ssem, q2_rsem,
):
    params, tiles, width = jac_hbm.shape
    me = lax.axis_index("track")
    my_det = lax.axis_index("det")
    per = tiles // n_track
    chunks = tiles // LANES

    load_jac = pltpu.make_async_copy(jac_hbm, jac_in, jac_sem)
    load_jac.start()

    def peer_of(step):
        return lax.rem(me + step, n_track)

    ahead = lax.rem(me + 1, n_track)
    behind = lax.rem(me + n_track - 1, n_track)

    barrier = pltpu.get_barrier_semaphore()

    def greet(step, carry):
        pl.semaphore_signal(barrier, inc=1, device_id=(peer_of(step), my_det), device_id_type=MESH)
        return carry

    lax.fori_loop(1, n_track, greet, 0)
    for off in range(1, n_det):
        other = lax.rem(my_det + off, n_det)
        for track in (me, ahead, behind):
            pl.semaphore_signal(barrier, inc=1, device_id=(track, other), device_id_type=MESH)

    match = match_ref[...]
    shift = tiles.bit_length() - 1
    dest = lax.shift_right_logical(match, jnp.full_like(match, shift))
    slot = jnp.bitwise_and(match, tiles - 1)
    own = iota((1, tiles), 1)
    same = 2 * jnp.minimum(own, slot) + jnp.where(own > slot, 1, 0)
    key = jnp.where(dest > me, own, jnp.where(dest < me, slot, same))
    full = (dest * (2 * tiles) + key).astype(F32)
    full_col = jnp.transpose(jnp.broadcast_to(full, (8, tiles)))[:, 0:1]
    place = jnp.zeros((1, tiles), F32)
    for c in range(chunks):
        less = jnp.where(full_col[c * LANES:(c + 1) * LANES] < full, 1.0, 0.0)
        place = place + jnp.sum(less, axis=0, keepdims=True)
    place_col = jnp.transpose(jnp.broadcast_to(place, (8, tiles)))[:, 0:1]
    for c in range(chunks):
        rows = slice(c * LANES, (c + 1) * LANES)
        row_no = (iota((LANES, tiles), 0) + c * LANES).astype(F32)
        sel_t[rows] = jnp.where(row_no == place, 1.0, 0.0).astype(BF16)
        lane_no = iota((LANES, tiles), 1).astype(F32)
        sel[rows] = jnp.where(lane_no == place_col[rows], 1.0, 0.0).astype(BF16)

    def pick(matrix, value):
        parts = jnp.concatenate(split3(value), axis=1)
        out = jnp.dot(matrix[...], parts, preferred_element_type=F32)
        w = value.shape[1]
        return (out[:, :w] + out[:, w:2 * w]) + out[:, 2 * w:]

    pred[0] = pick(sel_t, obs_ref[...])

    def exchange_start(r):
        mine = pred[r, pl.ds(pl.multiple_of(me * per, per), per), :]
        up = pltpu.roll(mine, per - 1, 0)
        down = pltpu.roll(mine, 1, 0)
        odd = jnp.bitwise_and(iota(mine.shape, 0), 1)
        arrived[r, pl.ds(pl.multiple_of(me * per, per), per), :] = jnp.where(odd == 1, down, up)

        def send(step, carry):
            peer = peer_of(step)
            pltpu.make_async_remote_copy(
                src_ref=pred.at[r, pl.ds(pl.multiple_of(peer * per, per), per), :],
                dst_ref=arrived.at[r, pl.ds(pl.multiple_of(me * per, per), per), :],
                send_sem=a_send.at[r], recv_sem=a_recv.at[r],
                device_id=(peer, my_det), device_id_type=MESH,
            ).start()
            return carry

        lax.fori_loop(1, n_track, send, 0)

    def wait_bytes(buffer, sem):
        pltpu.make_async_copy(buffer, buffer, sem).wait()

    def exchange_wait(r):
        wait_bytes(arrived.at[r, pl.ds(0, tiles - per), :], a_recv.at[r])

    def row_start(k, source, target, ssem, rsem):
        def send(step, carry):
            pltpu.make_async_remote_copy(
                src_ref=source.at[k], dst_ref=target.at[k, me],
                send_sem=ssem.at[k], recv_sem=rsem.at[k],
                device_id=(peer_of(step), my_det), device_id_type=MESH,
            ).start()
            return carry

        target[k, me] = source[k]
        lax.fori_loop(1, n_track, send, 0)

    def row_wait(k, target, rsem):
        wait_bytes(target.at[k, pl.ds(0, n_track - 1)], rsem.at[k])
        total = jnp.sum(target[k], axis=0)
        return jnp.sum(total, axis=1, keepdims=True)

    pl.semaphore_wait(barrier, (n_track - 1) + 3 * (n_det - 1))
    exchange_start(0)

    load_jac.wait()

    def order_jac(p, carry):
        jac_t[p] = jnp.transpose(pick(sel_t, jac_in[p]))
        return carry

    lax.fori_loop(0, params, order_jac, 0)
    frac_parts = [part.astype(F32) for part in split3(frac_ref[...])]
    table = jnp.concatenate([knot_ref[...].astype(F32)] + frac_parts + [jnp.zeros((ROWS - 4, tiles), F32)], axis=0)
    table = jnp.dot(table.astype(BF16), sel[...], preferred_element_type=F32)
    knot = table[0:1]
    frac = (table[1:2] + table[2:3]) + table[3:4]
    weight[0:1] = 1.0 - frac
    weight[1:2] = frac
    hot[...] = jnp.where(iota((LANES, tiles), 0).astype(F32) == knot, 1.0, 0.0).astype(BF16)
    spread_ref[...] = jnp.zeros_like(spread_ref)

    eye = iota((ROWS, LANES), 0) == iota((ROWS, LANES), 1)
    lane = iota((ROWS, LANES), 1)
    sub = iota((ROWS, LANES), 0)

    def to_row(col):
        return jnp.sum(jnp.where(eye, col, 0.0), axis=0, keepdims=True)

    def to_col(row):
        return jnp.sum(jnp.where(eye, row, 0.0), axis=1, keepdims=True)

    def adjoint_start(r):
        for c in range(chunks):
            cols = slice(c * LANES, (c + 1) * LANES)
            turned = jnp.transpose(upd_ref[cols, :])
            for p in range(params):
                spread_ref[p:p + 1, cols] = jnp.sum(jac_t[p, :, cols] * turned, axis=0, keepdims=True)
        sums = spread_ref[...]
        parts = split3(sums * weight[0:1]) + split3(sums * weight[1:2])
        out = lax.dot_general(
            jnp.concatenate(parts, axis=0), hot[...], (((1,), (1,)), ((), ())), preferred_element_type=F32
        )
        low = (out[0:16] + out[16:32]) + out[32:48]
        high = (out[48:64] + out[64:80]) + out[80:96]
        moved = pltpu.roll(high, 1, 1)
        spill = to_row(moved[:, 0:1])
        own_sum = low + jnp.where(lane > 0, moved, 0.0)
        first = to_row(own_sum[:, 0:1])
        own_sum = own_sum + jnp.where(sub == 12, spill, 0.0) + jnp.where(sub == 13, first, 0.0)
        det_send[r] = own_sum
        det_got[r, my_det] = own_sum
        for off in range(1, n_det):
            pltpu.make_async_remote_copy(
                src_ref=det_send.at[r], dst_ref=det_got.at[r, my_det],
                send_sem=d_send.at[r], recv_sem=d_recv.at[r],
                device_id=(me, lax.rem(my_det + off, n_det)), device_id_type=MESH,
            ).start()
        for off in range(n_det):
            other = lax.rem(my_det + off, n_det)
            for track, target, rsem in ((ahead, prev_got, e_recv), (behind, next_got, h_recv)):
                pltpu.make_async_remote_copy(
                    src_ref=det_send.at[r, pl.ds(8, 8), :], dst_ref=target.at[r, my_det],
                    send_sem=d_send.at[r], recv_sem=rsem.at[r],
                    device_id=(track, other), device_id_type=MESH,
                ).start()

    def adjoint_wait(r):
        wait_bytes(det_got.at[r, pl.ds(0, n_det - 1)], d_recv.at[r])
        wait_bytes(prev_got.at[r], e_recv.at[r])
        wait_bytes(next_got.at[r], h_recv.at[r])
        total = jnp.sum(det_got[r], axis=0)
        before = jnp.sum(prev_got[r], axis=0)[4:5]
        after = jnp.sum(next_got[r], axis=0)[5:6]
        carried = jnp.where(me > 0, to_col(before), 0.0)
        beyond = jnp.where(me < n_track - 1, to_col(total[12:13] + after), 0.0)
        main = jnp.where(sub < params, total, 0.0) + jnp.where(lane == 0, carried, 0.0)
        return jnp.concatenate([main, jnp.where(lane == 0, beyond, 0.0)], axis=1)

    def forward(r, field):
        later = pltpu.roll(field, 2 * LANES - 1, 1)
        parts = split3(field[:, :LANES]) + split3(later[:, :LANES])
        out = jnp.dot(jnp.concatenate(parts, axis=0), hot[...], preferred_element_type=F32)
        low = (out[0:16] + out[16:32]) + out[32:48]
        high = (out[48:64] + out[64:80]) + out[80:96]
        interp = low * weight[0:1] + high * weight[1:2]
        for c in range(chunks):
            cols = slice(c * LANES, (c + 1) * LANES)
            total = jac_t[0, :, cols] * interp[0:1, cols]
            for p in range(1, params):
                total = total + jac_t[p, :, cols] * interp[p:p + 1, cols]
            pred[r, cols, :] = jnp.transpose(total)

    exchange_wait(0)
    upd_ref[...] = pred[0] - arrived[0]
    r_ref[...] = upd_ref[...]
    adjoint_start(0)
    gradient = adjoint_wait(0)

    direction = swept = knots = None
    previous = None
    for k in range(ITERS):
        r = k + 1
        forward(r, gradient)
        exchange_start(r)
        squares = gradient[:, :LANES]
        gam_send[k] = jnp.sum(squares * squares, axis=0, keepdims=True)
        row_start(k, gam_send, gam_got, g_ssem, g_rsem)
        exchange_wait(r)
        norm = row_wait(k, gam_got, g_rsem)
        change = pred[r] - arrived[r]
        upd_ref[...] = change
        if k == 0:
            direction = gradient
        else:
            beta = norm / previous
            direction = gradient + beta * direction
            change = change + beta * fd_ref[...]
        fd_ref[...] = change
        held = direction[:, :LANES]
        partial = 0.5 * jnp.sum(change * change, axis=0, keepdims=True)
        partial = partial + (damping / n_det) * jnp.sum(held * held, axis=0, keepdims=True)
        q1_send[k] = partial
        q1_got[k, my_det] = partial
        for off in range(1, n_det):
            pltpu.make_async_remote_copy(
                src_ref=q1_send.at[k], dst_ref=q1_got.at[k, my_det],
                send_sem=q1_ssem.at[k], recv_sem=q1_rsem.at[k],
                device_id=(me, lax.rem(my_det + off, n_det)), device_id_type=MESH,
            ).start()
        if k < ITERS - 1:
            adjoint_start(r)
        wait_bytes(q1_got.at[k, pl.ds(0, n_det - 1)], q1_rsem.at[k])
        q2_send[k] = jnp.sum(q1_got[k], axis=0)
        row_start(k, q2_send, q2_got, q2_ssem, q2_rsem)
        if k < ITERS - 1:
            applied = adjoint_wait(r) + damping * gradient
            swept = applied if k == 0 else applied + beta * swept
        else:
            r_ref[...] = pick(sel, r_ref[...])
            upd_ref[...] = pick(sel, fd_ref[...])
        step = norm / row_wait(k, q2_got, q2_rsem)
        knots = step * direction if k == 0 else knots + step * direction
        if k < ITERS - 1:
            r_ref[...] = r_ref[...] - step * fd_ref[...]
            gradient = gradient - step * swept
            previous = norm
        else:
            r_out[...] = r_ref[...] - step * upd_ref[...]
    x_out[...] = knots[:params, :LANES]

    for r in range(ITERS + 1):
        wait_bytes(pred.at[r, pl.ds(0, tiles - per), :], a_send.at[r])
    for r in range(ITERS):
        wait_bytes(det_got.at[r, pl.ds(0, n_det - 1)], d_send.at[r])
        wait_bytes(prev_got.at[r], d_send.at[r])
        wait_bytes(next_got.at[r], d_send.at[r])
        wait_bytes(gam_got.at[r, pl.ds(0, n_track - 1)], g_ssem.at[r])
        wait_bytes(q1_got.at[r, pl.ds(0, n_det - 1)], q1_ssem.at[r])
        wait_bytes(q2_got.at[r, pl.ds(0, n_track - 1)], q2_ssem.at[r])


def local(n_track, n_det, jac, obs, match, tile_knot, tile_frac):
    tiles, params, width = jac.shape
    rounds = ITERS + 1
    dma = pltpu.SemaphoreType.DMA
    vmem = pl.BlockSpec(memory_space=pltpu.VMEM)
    row = (1, tiles)
    return pl.pallas_call(
        functools.partial(kernel, n_track, n_det),
        out_shape=(
            jax.ShapeDtypeStruct((params, KNOT_DEV), F32),
            jax.ShapeDtypeStruct((tiles, width), F32),
        ),
        in_specs=[pl.BlockSpec(memory_space=pl.ANY), vmem, vmem, vmem, vmem],
        out_specs=(vmem, vmem),
        scratch_shapes=[
            pltpu.VMEM((params, tiles, width), F32),
            pltpu.VMEM((params, width, tiles), F32),
            pltpu.VMEM((tiles, tiles), BF16),
            pltpu.VMEM((tiles, tiles), BF16),
            pltpu.VMEM((KNOT_DEV, tiles), BF16),
            pltpu.VMEM((8, tiles), F32),
            pltpu.VMEM((rounds, tiles, width), F32),
            pltpu.VMEM((rounds, tiles, width), F32),
            pltpu.VMEM((tiles, width), F32),
            pltpu.VMEM((tiles, width), F32),
            pltpu.VMEM((ROWS, tiles), F32),
            pltpu.VMEM((tiles, width), F32),
            pltpu.VMEM((ITERS, ROWS, KNOT_DEV), F32),
            pltpu.VMEM((ITERS, n_det, ROWS, KNOT_DEV), F32),
            pltpu.VMEM((ITERS, n_det, 8, KNOT_DEV), F32),
            pltpu.VMEM((ITERS, n_det, 8, KNOT_DEV), F32),
            pltpu.VMEM((ITERS, 1, LANES), F32),
            pltpu.VMEM((ITERS, n_track, 1, LANES), F32),
            pltpu.VMEM((ITERS, 1, LANES), F32),
            pltpu.VMEM((ITERS, n_det, 1, LANES), F32),
            pltpu.VMEM((ITERS, 1, LANES), F32),
            pltpu.VMEM((ITERS, n_track, 1, LANES), F32),
            dma, dma((rounds,)), dma((rounds,)),
            dma((ITERS,)), dma((ITERS,)), dma((ITERS,)), dma((ITERS,)),
            dma((ITERS,)), dma((ITERS,)), dma((ITERS,)), dma((ITERS,)), dma((ITERS,)), dma((ITERS,)),
        ],
        compiler_params=pltpu.CompilerParams(
            collective_id=0, has_side_effects=True, vmem_limit_bytes=48 * 1024 * 1024
        ),
    )(
        jnp.transpose(jac, (1, 0, 2)), obs,
        match.reshape(row), tile_knot.reshape(row), tile_frac.reshape(row),
    )


def solution(mesh):
    in_specs = (P("track", None, "det"), P("track", "det"), P("track"), P("track"), P("track"))
    out_specs = (P(None, "track"), P("track", "det"))
    body = functools.partial(local, mesh.shape["track"], mesh.shape["det"])
    return jax.shard_map(body, mesh=mesh, in_specs=in_specs, out_specs=out_specs, check_vma=False)
```

time: 1160 us -> 118 us (0.10)
  blocking collectives: 905 us -> 0 us
  Pallas kernels: 0 us -> 111 us
  starting transfers between devices: 78.6 us -> 0 us
  matrix products: 68.8 us -> 0 us
  other arithmetic: 33.7 us -> 0 us
  local copies, waits for them, and re-layouts: 33.2 us -> 6.18 us
  waiting for transfers between devices: 19.6 us -> 0 us
  between operations: 12.7 us -> 0.65 us
    psum x12 -> x0, blocking collectives: 854 us -> none  [the longest x4 490 us: slope_total(): return lax.psum(jnp.sum(gradient * gradient), 'track')]
    pallas_call x0 -> x1, Pallas kernels: none -> 111 us  [local(): pl.pallas_call(functools.partial(kernel, n_track, n_det), out_shape=(jax....]
    dot_general x20 -> x0, matrix products: 68.8 us -> none  [the longest x4 31.6 us: adjoint(): jnp.einsum('ipw,iw->pi', jac, residual_rows, precision=highest)]
    all_to_all x3 -> x0, blocking collectives: 51.5 us -> none  [partner_values(): lax.all_to_all(arrange(values), 'track', split_axis=0, concat_axis=0, til...]
    ppermute x8 -> x0, starting transfers between devices: 51 us -> none  [passed_along(): lax.ppermute(value, axis, [(source, source + steps) for source in range(l...]
    all_to_all x3 -> x0, starting transfers between devices: 27.7 us -> none  [the longest x2 14.5 us: partner_values(): lax.all_to_all(arrange(values), 'track', split_axis=0, concat_axis=0, til...]
    gather x11 -> x0, local copies, waits for them, and re-layouts: 24.7 us -> none  [the longest x5 12.9 us: settle(): return joined[receive_order]]
    reduce_sum x11 -> x0, other arithmetic: 13.7 us -> none  [the longest x4 9.3 us: local(): jnp.sum(change * change)]
  transfers between devices with their start and end apart: 11 -> 0, of which waited for: 9 -> 0; matrix products, arithmetic and copies ran while one was open for 1% -> 0% of each run, Pallas kernels for 0% -> 0%
where the time goes in v1:
time: 118 us
  Pallas kernels  111 us (94%)
  local copies, waits for them, and re-layouts  6.18 us (5%)
    pallas_call x1, Pallas kernels, local(): pl.pallas_call(functools.partial(kernel, n_track, n_det), out_shape=(jax....  111 us
    unnamed x12, local copies, waits for them, and re-layouts  6.18 us

profile of v1, /device:TPU:1, one launch (start us, length us, event | category | flops | bytes accessed | tf_op | source)
XLA Modules:
  0.0 117.8 jit_solution(10865635139956189247)
XLA Ops:
  0.6 0.0 copy-start
  0.6 1.9 %copy-done = f32[512,12,128]{2,0,1:T(8,128)S(1)} copy-done((f32[512,12,128]{2,0,1:T(8,128)S(1)}, f32[512,12,128]{2,0,1:T(8,128)}, u32[]{:S(2)}) %copy-start) | copy-done | bytes 3145752
  2.5 0.0 copy-start.1
  2.5 0.9 copy-done.1
  3.5 0.0 copy-start.2
  3.5 0.7 copy-done.2
  4.2 0.0 copy-start.3
  4.2 0.7 copy-done.3
  4.8 0.0 copy-start.4
  4.8 0.7 copy-done.4
  5.5 111.0 %shard_map.68 = (f32[12,128]{1,0:T(8,128)S(1)}, f32[512,128]{1,0:T(8,128)S(1)}) custom-call(f32[12,512,128]{2,1,0:T(8,128)S(1)} %bitcast.4, f32[512,128]{1,0:T(8,128)S(1)} %copy-done.1, s32[1,512]{1,0:T(1,128)S(1)} %bitcast.5, s32[1,512]{1,0:T(1,128)S(1)} %bitcast.6, f32[1,512]{1,0:T(1,128)S(1)} %bitcast.7), custom_call_target="tpu_custom_call" | custom-call | tf_op jit(solution)/shard_map/pallas_call | solution.py:305
  116.5 0.6 copy.9
  117.1 0.7 copy.10
Async XLA Ops:
  0.6 1.9 %copy-start = (f32[512,12,128]{2,0,1:T(8,128)S(1)}, f32[512,12,128]{2,0,1:T(8,128)}, u32[]{:S(2)}) copy-start(f32[512,12,128]{2,0,1:T(8,128)} %param.5) | copy-start | bytes 9437188
  2.5 0.9 copy-start.1
  3.5 0.7 copy-start.2
  4.2 0.7 copy-start.3
  4.8 0.7 copy-start.4

commit v2 on v1

--- a/solution.py
+++ b/solution.py
@@ -12,6 +12,7 @@
 LANES = 128
 ROWS = 16
 MESH = pl.DeviceIdType.MESH
+TRACK_DIMS = (4, 8, 2)
 F32 = jnp.float32
 BF16 = jnp.bfloat16
 
@@ -32,11 +33,12 @@
 
 def kernel(
     n_track, n_det,
-    jac_hbm, obs_ref, match_ref, knot_ref, frac_ref,
+    jac_hbm, obs_hbm, match_hbm, knot_hbm, frac_hbm,
     x_out, r_out,
-    jac_in, jac_t, sel, sel_t, hot, weight, pred, arrived, fd_ref, r_ref, spread_ref, upd_ref,
+    obs_ref, match_ref, knot_ref, frac_ref,
+    jac_in, jac_t, sel, sel_t, hot, weight, pred, arrived, fd_ref, r_ref, spread_ref, fg_ref,
     det_send, det_got, prev_got, next_got, gam_send, gam_got, q1_send, q1_got, q2_send, q2_got,
-    jac_sem, a_send, a_recv, d_send, d_recv, e_recv, h_recv, g_ssem, g_rsem, q1_ssem, q1_rsem, q2_ssem, q2_rsem,
+    in_sem, jac_sem, a_send, a_recv, d_send, d_recv, e_recv, h_recv, g_ssem, g_rsem, q1_ssem, q1_rsem, q2_ssem, q2_rsem,
 ):
     params, tiles, width = jac_hbm.shape
     me = lax.axis_index("track")
@@ -44,11 +46,35 @@
     per = tiles // n_track
     chunks = tiles // LANES
 
+    loads = [
+        pltpu.make_async_copy(source, target, in_sem.at[i])
+        for i, (source, target) in enumerate(
+            ((match_hbm, match_ref), (knot_hbm, knot_ref), (frac_hbm, frac_ref), (obs_hbm, obs_ref))
+        )
+    ]
+    for load in loads:
+        load.start()
     load_jac = pltpu.make_async_copy(jac_hbm, jac_in, jac_sem)
     load_jac.start()
 
+    def far_first(index, count):
+        half = lax.div(index + 1, 2)
+        return lax.rem(count // 2 + half * (1 - 2 * lax.rem(index, 2)) + count, count)
+
+    def far_first_py(index, count):
+        half = (index + 1) // 2
+        return (count // 2 + half * (1 - 2 * (index % 2))) % count
+
+    n_y, n_z, n_core = TRACK_DIMS
+    my_y = lax.div(me, n_z * n_core)
+    my_z = lax.rem(lax.div(me, n_core), n_z)
+    my_core = lax.rem(me, n_core)
+
     def peer_of(step):
-        return lax.rem(me + step, n_track)
+        y = lax.rem(my_y + far_first(lax.div(step, n_z * n_core), n_y), n_y)
+        z = lax.rem(my_z + far_first(lax.rem(lax.div(step, n_core), n_z), n_z), n_z)
+        core = lax.rem(my_core + n_core - 1 - lax.rem(step, n_core), n_core)
+        return (y * n_z + z) * n_core + core
 
     ahead = lax.rem(me + 1, n_track)
     behind = lax.rem(me + n_track - 1, n_track)
@@ -59,12 +85,14 @@
         pl.semaphore_signal(barrier, inc=1, device_id=(peer_of(step), my_det), device_id_type=MESH)
         return carry
 
-    lax.fori_loop(1, n_track, greet, 0)
+    lax.fori_loop(0, n_track - 1, greet, 0)
     for off in range(1, n_det):
         other = lax.rem(my_det + off, n_det)
         for track in (me, ahead, behind):
             pl.semaphore_signal(barrier, inc=1, device_id=(track, other), device_id_type=MESH)
 
+    for load in loads:
+        load.wait()
     match = match_ref[...]
     shift = tiles.bit_length() - 1
     dest = lax.shift_right_logical(match, jnp.full_like(match, shift))
@@ -103,21 +131,27 @@
 
         def send(step, carry):
             peer = peer_of(step)
+            group = lax.div(step, n_z * n_core)
             pltpu.make_async_remote_copy(
                 src_ref=pred.at[r, pl.ds(pl.multiple_of(peer * per, per), per), :],
                 dst_ref=arrived.at[r, pl.ds(pl.multiple_of(me * per, per), per), :],
-                send_sem=a_send.at[r], recv_sem=a_recv.at[r],
+                send_sem=a_send.at[r], recv_sem=a_recv.at[r, group],
                 device_id=(peer, my_det), device_id_type=MESH,
             ).start()
             return carry
 
-        lax.fori_loop(1, n_track, send, 0)
+        lax.fori_loop(0, n_track - 1, send, 0)
 
     def wait_bytes(buffer, sem):
         pltpu.make_async_copy(buffer, buffer, sem).wait()
 
-    def exchange_wait(r):
-        wait_bytes(arrived.at[r, pl.ds(0, tiles - per), :], a_recv.at[r])
+    def exchange_groups(r):
+        for group in range(n_y):
+            y = lax.rem(my_y + n_y - far_first_py(group, n_y), n_y)
+            rows = pl.ds(pl.multiple_of(y * LANES, LANES), LANES)
+            count = LANES if group < n_y - 1 else LANES - per
+            wait_bytes(arrived.at[r, pl.ds(0, count), :], a_recv.at[r, group])
+            yield rows
 
     def row_start(k, source, target, ssem, rsem):
         def send(step, carry):
@@ -129,12 +163,11 @@
             return carry
 
         target[k, me] = source[k]
-        lax.fori_loop(1, n_track, send, 0)
+        lax.fori_loop(0, n_track - 1, send, 0)
 
     def row_wait(k, target, rsem):
         wait_bytes(target.at[k, pl.ds(0, n_track - 1)], rsem.at[k])
-        total = jnp.sum(target[k], axis=0)
-        return jnp.sum(total, axis=1, keepdims=True)
+        return jnp.sum(jnp.sum(target[k], axis=0), axis=1, keepdims=True)
 
     pl.semaphore_wait(barrier, (n_track - 1) + 3 * (n_det - 1))
     exchange_start(0)
@@ -166,12 +199,12 @@
     def to_col(row):
         return jnp.sum(jnp.where(eye, row, 0.0), axis=1, keepdims=True)
 
+    def adjoint_part(cols, values):
+        turned = jnp.transpose(values)
+        for p in range(params):
+            spread_ref[p:p + 1, cols] = jnp.sum(jac_t[p, :, cols] * turned, axis=0, keepdims=True)
+
     def adjoint_start(r):
-        for c in range(chunks):
-            cols = slice(c * LANES, (c + 1) * LANES)
-            turned = jnp.transpose(upd_ref[cols, :])
-            for p in range(params):
-                spread_ref[p:p + 1, cols] = jnp.sum(jac_t[p, :, cols] * turned, axis=0, keepdims=True)
         sums = spread_ref[...]
         parts = split3(sums * weight[0:1]) + split3(sums * weight[1:2])
         out = lax.dot_general(
@@ -227,35 +260,42 @@
                 total = total + jac_t[p, :, cols] * interp[p:p + 1, cols]
             pred[r, cols, :] = jnp.transpose(total)
 
-    exchange_wait(0)
-    upd_ref[...] = pred[0] - arrived[0]
-    r_ref[...] = upd_ref[...]
+    for rows in exchange_groups(0):
+        misfit = pred[0, rows, :] - arrived[0, rows, :]
+        r_ref[rows, :] = misfit
+        adjoint_part(rows, misfit)
     adjoint_start(0)
     gradient = adjoint_wait(0)
-
-    direction = swept = knots = None
-    previous = None
+    forward(1, gradient)
+    exchange_start(1)
+
+    def norm_start(k, field):
+        main = field[:, :LANES]
+        gam_send[k] = jnp.sum(main * main, axis=0, keepdims=True)
+        row_start(k, gam_send, gam_got, g_ssem, g_rsem)
+
+    norm_start(0, gradient)
+    direction = swept = knots = norm = curve = step = None
     for k in range(ITERS):
         r = k + 1
-        forward(r, gradient)
-        exchange_start(r)
-        squares = gradient[:, :LANES]
-        gam_send[k] = jnp.sum(squares * squares, axis=0, keepdims=True)
-        row_start(k, gam_send, gam_got, g_ssem, g_rsem)
-        exchange_wait(r)
-        norm = row_wait(k, gam_got, g_rsem)
-        change = pred[r] - arrived[r]
-        upd_ref[...] = change
-        if k == 0:
-            direction = gradient
-        else:
-            beta = norm / previous
-            direction = gradient + beta * direction
-            change = change + beta * fd_ref[...]
-        fd_ref[...] = change
-        held = direction[:, :LANES]
-        partial = 0.5 * jnp.sum(change * change, axis=0, keepdims=True)
-        partial = partial + (damping / n_det) * jnp.sum(held * held, axis=0, keepdims=True)
+        last = k == ITERS - 1
+        own_part = jnp.zeros((1, LANES), F32)
+        cross_part = jnp.zeros((1, LANES), F32)
+        for rows in exchange_groups(r):
+            change = pred[r, rows, :] - arrived[r, rows, :]
+            if k > 0:
+                change = fg_ref[rows, :] - step * change
+                cross_part = cross_part + 0.5 * jnp.sum(change * fd_ref[rows, :], axis=0, keepdims=True)
+            fg_ref[rows, :] = change
+            own_part = own_part + 0.5 * jnp.sum(change * change, axis=0, keepdims=True)
+            if not last:
+                adjoint_part(rows, change)
+        main = gradient[:, :LANES]
+        share = damping / n_det
+        own_part = own_part + share * jnp.sum(main * main, axis=0, keepdims=True)
+        if k > 0:
+            cross_part = cross_part + share * jnp.sum(main * direction[:, :LANES], axis=0, keepdims=True)
+        partial = jnp.concatenate([own_part, cross_part], axis=0)
         q1_send[k] = partial
         q1_got[k, my_det] = partial
         for off in range(1, n_det):
@@ -264,25 +304,38 @@
                 send_sem=q1_ssem.at[k], recv_sem=q1_rsem.at[k],
                 device_id=(me, lax.rem(my_det + off, n_det)), device_id_type=MESH,
             ).start()
-        if k < ITERS - 1:
+        if not last:
             adjoint_start(r)
+        new_norm = row_wait(k, gam_got, g_rsem)
+        if k == 0:
+            direction = gradient
+            fd_ref[...] = fg_ref[...]
+        else:
+            beta = new_norm / norm
+            direction = gradient + beta * direction
+            fd_ref[...] = fg_ref[...] + beta * fd_ref[...]
+        norm = new_norm
         wait_bytes(q1_got.at[k, pl.ds(0, n_det - 1)], q1_rsem.at[k])
         q2_send[k] = jnp.sum(q1_got[k], axis=0)
         row_start(k, q2_send, q2_got, q2_ssem, q2_rsem)
-        if k < ITERS - 1:
+        if not last:
             applied = adjoint_wait(r) + damping * gradient
             swept = applied if k == 0 else applied + beta * swept
+            forward(r + 1, swept)
+            exchange_start(r + 1)
         else:
             r_ref[...] = pick(sel, r_ref[...])
-            upd_ref[...] = pick(sel, fd_ref[...])
-        step = norm / row_wait(k, q2_got, q2_rsem)
+            fg_ref[...] = pick(sel, fd_ref[...])
+        sums = row_wait(k, q2_got, q2_rsem)
+        curve = sums[0:1] if k == 0 else sums[0:1] + beta * (2.0 * sums[1:2] + beta * curve)
+        step = norm / curve
         knots = step * direction if k == 0 else knots + step * direction
-        if k < ITERS - 1:
+        if not last:
+            gradient = gradient - step * swept
+            norm_start(k + 1, gradient)
             r_ref[...] = r_ref[...] - step * fd_ref[...]
-            gradient = gradient - step * swept
-            previous = norm
         else:
-            r_out[...] = r_ref[...] - step * upd_ref[...]
+            r_out[...] = r_ref[...] - step * fg_ref[...]
     x_out[...] = knots[:params, :LANES]
 
     for r in range(ITERS + 1):
@@ -308,9 +361,13 @@
             jax.ShapeDtypeStruct((params, KNOT_DEV), F32),
             jax.ShapeDtypeStruct((tiles, width), F32),
         ),
-        in_specs=[pl.BlockSpec(memory_space=pl.ANY), vmem, vmem, vmem, vmem],
+        in_specs=[pl.BlockSpec(memory_space=pltpu.HBM)] * 5,
         out_specs=(vmem, vmem),
         scratch_shapes=[
+            pltpu.VMEM((tiles, width), F32),
+            pltpu.VMEM(row, jnp.int32),
+            pltpu.VMEM(row, jnp.int32),
+            pltpu.VMEM(row, F32),
             pltpu.VMEM((params, tiles, width), F32),
             pltpu.VMEM((params, width, tiles), F32),
             pltpu.VMEM((tiles, tiles), BF16),
@@ -329,16 +386,16 @@
             pltpu.VMEM((ITERS, n_det, 8, KNOT_DEV), F32),
             pltpu.VMEM((ITERS, 1, LANES), F32),
             pltpu.VMEM((ITERS, n_track, 1, LANES), F32),
-            pltpu.VMEM((ITERS, 1, LANES), F32),
-            pltpu.VMEM((ITERS, n_det, 1, LANES), F32),
-            pltpu.VMEM((ITERS, 1, LANES), F32),
-            pltpu.VMEM((ITERS, n_track, 1, LANES), F32),
-            dma, dma((rounds,)), dma((rounds,)),
+            pltpu.VMEM((ITERS, 2, LANES), F32),
+            pltpu.VMEM((ITERS, n_det, 2, LANES), F32),
+            pltpu.VMEM((ITERS, 2, LANES), F32),
+            pltpu.VMEM((ITERS, n_track, 2, LANES), F32),
+            dma((4,)), dma, dma((rounds,)), dma((rounds, TRACK_DIMS[0])),
             dma((ITERS,)), dma((ITERS,)), dma((ITERS,)), dma((ITERS,)),
             dma((ITERS,)), dma((ITERS,)), dma((ITERS,)), dma((ITERS,)), dma((ITERS,)), dma((ITERS,)),
         ],
         compiler_params=pltpu.CompilerParams(
-            collective_id=0, has_side_effects=True, vmem_limit_bytes=48 * 1024 * 1024
+            collective_id=0, has_side_effects=True, vmem_limit_bytes=67043328
         ),
     )(
         jnp.transpose(jac, (1, 0, 2)), obs,

time: 118 us -> 95.1 us (0.81)
  Pallas kernels: 111 us -> 91.3 us
  local copies, waits for them, and re-layouts: 6.18 us -> 2.96 us
    pallas_call x1, Pallas kernels: 111 us -> 91.3 us  [local(): pl.pallas_call(functools.partial(kernel, n_track, n_det), out_shape=(jax....]
    unnamed x12 -> x2, local copies, waits for them, and re-layouts: 6.18 us -> 2.96 us
where the time goes in v2:
time: 95.1 us; the launch traced here: 94.9 us
  Pallas kernels  91.3 us (96%)
  local copies, waits for them, and re-layouts  2.96 us (3%)
    pallas_call x1, Pallas kernels, local(): pl.pallas_call(functools.partial(kernel, n_track, n_det), out_shape=(jax....  91.3 us
    unnamed x2, local copies, waits for them, and re-layouts  2.96 us

profile of v2, /device:TPU:1, one launch (start us, length us, event | category | flops | bytes accessed | tf_op | source)
XLA Modules:
  0.0 94.9 jit_solution(4282727880530257571)
XLA Ops:
  0.6 91.3 %shard_map.68 = (f32[12,128]{1,0:T(8,128)}, f32[512,128]{1,0:T(8,128)}) custom-call(f32[12,512,128]{2,1,0:T(8,128)} %bitcast.4, f32[512,128]{1,0:T(8,128)} %obs_hbm.1, s32[1,512]{1,0:T(1,128)} %bitcast.5, s32[1,512]{1,0:T(1,128)} %bitcast.6, f32[1,512]{1,0:T(1,128)} %bitcast.7), custom_call_target="tpu_custom_call" | custom-call | tf_op jit(solution)/shard_map/pallas_call | solution.py:358
  92.0 1.3 %copy.9 = f32[12,128]{1,0:T(8,128)} copy(f32[12,128]{1,0:T(8,128)} %get-tuple-element.4) | data formatting | bytes 12288
  93.3 1.7 %copy.10 = f32[512,128]{1,0:T(8,128)} copy(f32[512,128]{1,0:T(8,128)} %get-tuple-element.5) | data formatting | bytes 524288

commit v3 on v2

v3 whole, which is shorter than its diff:
```python
import functools

import jax
import jax.numpy as jnp
from jax import lax
from jax.experimental import pallas as pl
from jax.experimental.pallas import tpu as pltpu
from jax.sharding import PartitionSpec as P

KNOT_DEV = 128
ITERS = 4
LANES = 128
ROWS = 16
MESH = pl.DeviceIdType.MESH
TRACK_DIMS = (4, 8, 2)
F32 = jnp.float32
BF16 = jnp.bfloat16

damping = 1.0


def split3(value):
    high = value.astype(BF16)
    rest = value - high.astype(F32)
    mid = rest.astype(BF16)
    low = (rest - mid.astype(F32)).astype(BF16)
    return high, mid, low


def iota(shape, dim):
    return lax.broadcasted_iota(jnp.int32, shape, dim)


def kernel(
    n_track, n_det,
    jac_hbm, obs_hbm, match_hbm, knot_hbm, frac_hbm,
    x_out, r_out,
    obs_ref, match_ref, knot_ref, frac_ref,
    jac_in, jac_t, sel, sel_t, hot, weight, pred, arrived, fd_ref, r_ref, spread_ref, interp_ref, fg_ref,
    det_send, det_got, edge_send, prev_got, next_got,
    g1_send, g1_got, g2_send, g2_got, q1_send, q1_got, q2_send, q2_got,
    in_sem, jac_sem, a_send, a_recv, d_send, d_recv, e_send, e_recv, h_recv,
    g1_ssem, g1_rsem, g2_ssem, g2_rsem, q1_ssem, q1_rsem, q2_ssem, q2_rsem,
):
    params, tiles, width = jac_hbm.shape
    me = lax.axis_index("track")
    my_det = lax.axis_index("det")
    per = tiles // n_track
    chunks = tiles // LANES

    def far_first(index, count):
        half = lax.div(index + 1, 2)
        return lax.rem(count // 2 + half * (1 - 2 * lax.rem(index, 2)) + count, count)

    def far_first_py(index, count):
        half = (index + 1) // 2
        return (count // 2 + half * (1 - 2 * (index % 2))) % count

    n_y, n_z, n_core = TRACK_DIMS
    my_y = lax.div(me, n_z * n_core)
    my_z = lax.rem(lax.div(me, n_core), n_z)
    my_core = lax.rem(me, n_core)

    def peer_of(step):
        y = lax.rem(my_y + far_first(lax.div(step, n_z * n_core), n_y), n_y)
        z = lax.rem(my_z + far_first(lax.rem(lax.div(step, n_core), n_z), n_z), n_z)
        core = lax.rem(my_core + n_core - 1 - lax.rem(step, n_core), n_core)
        return (y * n_z + z) * n_core + core

    ahead = lax.rem(me + 1, n_track)
    behind = lax.rem(me + n_track - 1, n_track)

    others_y = [lax.rem(my_y + far_first_py(i, n_y), n_y) for i in range(n_y - 1)]
    others_det = [lax.rem(my_det + far_first_py(i, n_det), n_det) for i in range(n_det - 1)]

    def at(y, z, core):
        return (y * n_z + z) * n_core + core

    peers_y = [(at(y, my_z, my_core), my_det) for y in others_y]
    peers_x = [(me, det) for det in others_det]
    peers_xy = [(at(y, my_z, my_core), det) for y in others_y for det in others_det] + peers_y + peers_x
    peers_z = [
        (at(my_y, lax.rem(my_z + far_first_py(i, n_z), n_z), lax.rem(my_core + core, n_core)), my_det)
        for i in range(n_z) for core in reversed(range(n_core)) if i < n_z - 1 or core > 0
    ]
    edges = [(track, det) for track in (ahead, behind) for det in others_det + [my_det]]

    barrier = pltpu.get_barrier_semaphore()

    def greet(step, carry):
        pl.semaphore_signal(barrier, inc=1, device_id=(peer_of(step), my_det), device_id_type=MESH)
        return carry

    lax.fori_loop(0, n_track - 1, greet, 0)
    cross = len(peers_xy) - len(peers_y)
    for device in peers_xy[:cross - len(peers_x)] + peers_x + edges[:n_det - 1] + edges[n_det:2 * n_det - 1]:
        pl.semaphore_signal(barrier, inc=1, device_id=device, device_id_type=MESH)

    loads = [
        pltpu.make_async_copy(source, target, in_sem.at[i])
        for i, (source, target) in enumerate(
            ((match_hbm, match_ref), (knot_hbm, knot_ref), (frac_hbm, frac_ref), (obs_hbm, obs_ref))
        )
    ]
    for load in loads:
        load.start()
    load_jac = pltpu.make_async_copy(jac_hbm, jac_in, jac_sem)
    load_jac.start()

    for load in loads:
        load.wait()
    match = match_ref[...]
    shift = tiles.bit_length() - 1
    dest = lax.shift_right_logical(match, jnp.full_like(match, shift))
    slot = jnp.bitwise_and(match, tiles - 1)
    own = iota((1, tiles), 1)
    same = 2 * jnp.minimum(own, slot) + jnp.where(own > slot, 1, 0)
    key = jnp.where(dest > me, own, jnp.where(dest < me, slot, same))
    full = (dest * (2 * tiles) + key).astype(F32)
    full_col = jnp.transpose(jnp.broadcast_to(full, (8, tiles)))[:, 0:1]
    place = jnp.zeros((1, tiles), F32)
    for c in range(chunks):
        less = jnp.where(full_col[c * LANES:(c + 1) * LANES] < full, 1.0, 0.0)
        place = place + jnp.sum(less, axis=0, keepdims=True)
    place_col = jnp.transpose(jnp.broadcast_to(place, (8, tiles)))[:, 0:1]
    for c in range(chunks):
        rows = slice(c * LANES, (c + 1) * LANES)
        row_no = (iota((LANES, tiles), 0) + c * LANES).astype(F32)
        sel_t[rows] = jnp.where(row_no == place, 1.0, 0.0).astype(BF16)
        lane_no = iota((LANES, tiles), 1).astype(F32)
        sel[rows] = jnp.where(lane_no == place_col[rows], 1.0, 0.0).astype(BF16)

    def pick(matrix, value):
        parts = jnp.concatenate(split3(value), axis=1)
        out = jnp.dot(matrix[...], parts, preferred_element_type=F32)
        w = value.shape[1]
        return (out[:, :w] + out[:, w:2 * w]) + out[:, 2 * w:]

    pred[0] = pick(sel_t, obs_ref[...])

    per_y = n_z * n_core

    def exchange_start(r, group):
        if group == n_y - 1:
            here = pl.ds(pl.multiple_of(me * per, per), per)
            mine = pred[r, here, :]
            up = pltpu.roll(mine, per - 1, 0)
            down = pltpu.roll(mine, 1, 0)
            odd = jnp.bitwise_and(iota(mine.shape, 0), 1)
            arrived[r, here, :] = jnp.where(odd == 1, down, up)

        def send(step, carry):
            peer = peer_of(step)
            pltpu.make_async_remote_copy(
                src_ref=pred.at[r, pl.ds(pl.multiple_of(peer * per, per), per), :],
                dst_ref=arrived.at[r, pl.ds(pl.multiple_of(me * per, per), per), :],
                send_sem=a_send.at[r], recv_sem=a_recv.at[r, group],
                device_id=(peer, my_det), device_id_type=MESH,
            ).start()
            return carry

        lax.fori_loop(group * per_y, min(group * per_y + per_y, n_track - 1), send, 0)

    def wait_bytes(buffer, sem):
        pltpu.make_async_copy(buffer, buffer, sem).wait()

    def exchange_groups(r):
        for group in range(n_y):
            y = lax.rem(my_y + n_y - far_first_py(group, n_y), n_y)
            rows = pl.ds(pl.multiple_of(y * LANES, LANES), LANES)
            count = LANES if group < n_y - 1 else LANES - per
            wait_bytes(arrived.at[r, pl.ds(0, count), :], a_recv.at[r, group])
            yield rows

    def send_rows(k, source, target, slot, ssem, rsem, peers):
        target[k, slot] = source[k]
        for device in peers:
            pltpu.make_async_remote_copy(
                src_ref=source.at[k], dst_ref=target.at[k, slot],
                send_sem=ssem.at[k], recv_sem=rsem.at[k],
                device_id=device, device_id_type=MESH,
            ).start()

    def add_rows(k, target, rsem):
        wait_bytes(target.at[k, pl.ds(0, target.shape[1] - 1)], rsem.at[k])
        return jnp.sum(target[k], axis=0)

    slot_z = my_z * n_core + my_core

    pl.semaphore_wait(barrier, (n_track - 1) + cross + 2 * (n_det - 1))
    for group in range(n_y):
        exchange_start(0, group)

    load_jac.wait()

    def order_jac(p, carry):
        jac_t[p] = jnp.transpose(pick(sel_t, jac_in[p]))
        return carry

    lax.fori_loop(0, params, order_jac, 0)
    frac_parts = [part.astype(F32) for part in split3(frac_ref[...])]
    table = jnp.concatenate([knot_ref[...].astype(F32)] + frac_parts + [jnp.zeros((ROWS - 4, tiles), F32)], axis=0)
    table = jnp.dot(table.astype(BF16), sel[...], preferred_element_type=F32)
    knot = table[0:1]
    frac = (table[1:2] + table[2:3]) + table[3:4]
    weight[0:1] = 1.0 - frac
    weight[1:2] = frac
    weight[2:3] = jnp.where(knot == KNOT_DEV - 1, frac, 0.0)
    weight[3:4] = jnp.where(knot == 0, 1.0 - frac, 0.0)
    hot[...] = jnp.where(iota((LANES, tiles), 0).astype(F32) == knot, 1.0, 0.0).astype(BF16)
    spread_ref[...] = jnp.zeros_like(spread_ref)

    eye = iota((ROWS, LANES), 0) == iota((ROWS, LANES), 1)
    lane = iota((ROWS, LANES), 1)
    sub = iota((ROWS, LANES), 0)

    def to_row(col):
        return jnp.sum(jnp.where(eye, col, 0.0), axis=0, keepdims=True)

    def to_col(row):
        return jnp.sum(jnp.where(eye, row, 0.0), axis=1, keepdims=True)

    def adjoint_part(cols, values):
        turned = jnp.transpose(values)
        for p in range(params):
            spread_ref[p:p + 1, cols] = jnp.sum(jac_t[p, :, cols] * turned, axis=0, keepdims=True)

    def adjoint_start(r):
        sums = spread_ref[...]
        spill = to_row(jnp.sum(sums * weight[2:3], axis=1, keepdims=True))
        first_col = jnp.sum(sums * weight[3:4], axis=1, keepdims=True)
        edge_send[r, 0] = spill
        edge_send[r, 1] = to_row(first_col)
        for side, target, rsem in ((0, prev_got, e_recv), (1, next_got, h_recv)):
            for device in edges[side * n_det:(side + 1) * n_det]:
                pltpu.make_async_remote_copy(
                    src_ref=edge_send.at[r, side], dst_ref=target.at[r, my_det],
                    send_sem=e_send.at[r], recv_sem=rsem.at[r],
                    device_id=device, device_id_type=MESH,
                ).start()
        parts = split3(sums * weight[0:1]) + split3(sums * weight[1:2])
        out = lax.dot_general(
            jnp.concatenate(parts, axis=0), hot[...], (((1,), (1,)), ((), ())), preferred_element_type=F32
        )
        low = (out[0:16] + out[16:32]) + out[32:48]
        high = (out[48:64] + out[64:80]) + out[80:96]
        own_sum = jnp.where(lane > 0, low + pltpu.roll(high, 1, 1), first_col)
        own_sum = own_sum + jnp.where(sub == params, spill, 0.0)
        det_send[r] = own_sum
        det_got[r, my_det] = own_sum
        for device in peers_x:
            pltpu.make_async_remote_copy(
                src_ref=det_send.at[r], dst_ref=det_got.at[r, my_det],
                send_sem=d_send.at[r], recv_sem=d_recv.at[r],
                device_id=device, device_id_type=MESH,
            ).start()

    def adjoint_wait(r):
        wait_bytes(det_got.at[r, pl.ds(0, n_det - 1)], d_recv.at[r])
        wait_bytes(prev_got.at[r], e_recv.at[r])
        wait_bytes(next_got.at[r], h_recv.at[r])
        total = jnp.sum(det_got[r], axis=0)
        before = jnp.sum(prev_got[r], axis=0)
        after = jnp.sum(next_got[r], axis=0)
        carried = jnp.where(me > 0, to_col(before), 0.0)
        beyond = jnp.where(me < n_track - 1, to_col(total[params:params + 1] + after), 0.0)
        main = jnp.where(sub < params, total, 0.0) + jnp.where(lane == 0, carried, 0.0)
        return jnp.concatenate([main, jnp.where(lane == 0, beyond, 0.0)], axis=1)

    def forward(r, field):
        later = pltpu.roll(field, 2 * LANES - 1, 1)
        parts = split3(field[:, :LANES]) + split3(later[:, :LANES])
        out = jnp.dot(jnp.concatenate(parts, axis=0), hot[...], preferred_element_type=F32)
        low = (out[0:16] + out[16:32]) + out[32:48]
        high = (out[48:64] + out[64:80]) + out[80:96]
        interp_ref[...] = low * weight[0:1] + high * weight[1:2]
        for group in range(n_y):
            y = lax.rem(my_y + far_first_py(group, n_y), n_y)
            cols = pl.ds(pl.multiple_of(y * LANES, LANES), LANES)
            total = jac_t[0, :, cols] * interp_ref[0:1, cols]
            for p in range(1, params):
                total = total + jac_t[p, :, cols] * interp_ref[p:p + 1, cols]
            pred[r, cols, :] = jnp.transpose(total)
            exchange_start(r, group)

    for rows in exchange_groups(0):
        misfit = pred[0, rows, :] - arrived[0, rows, :]
        r_ref[rows, :] = misfit
        adjoint_part(rows, misfit)
    adjoint_start(0)
    gradient = adjoint_wait(0)
    forward(1, gradient)

    def norm_start(k, field):
        main = field[:, :LANES]
        g1_send[k] = jnp.sum(main * main, axis=0, keepdims=True)
        send_rows(k, g1_send, g1_got, my_y, g1_ssem, g1_rsem, peers_y)

    def norm_pass(k):
        g2_send[k] = add_rows(k, g1_got, g1_rsem)
        send_rows(k, g2_send, g2_got, slot_z, g2_ssem, g2_rsem, peers_z)

    norm_start(0, gradient)
    direction = swept = knots = norm = curve = step = None
    for k in range(ITERS):
        r = k + 1
        norm_pass(k)
        last = k == ITERS - 1
        own_part = jnp.zeros((1, LANES), F32)
        cross_part = jnp.zeros((1, LANES), F32)
        for rows in exchange_groups(r):
            change = pred[r, rows, :] - arrived[r, rows, :]
            if k > 0:
                change = fg_ref[rows, :] - step * change
                cross_part = cross_part + 0.5 * jnp.sum(change * fd_ref[rows, :], axis=0, keepdims=True)
            fg_ref[rows, :] = change
            own_part = own_part + 0.5 * jnp.sum(change * change, axis=0, keepdims=True)
            if not last:
                adjoint_part(rows, change)
        main = gradient[:, :LANES]
        share = damping / n_det
        own_part = own_part + share * jnp.sum(main * main, axis=0, keepdims=True)
        if k > 0:
            cross_part = cross_part + share * jnp.sum(main * direction[:, :LANES], axis=0, keepdims=True)
        partial = jnp.concatenate([own_part, cross_part], axis=0)
        q1_send[k] = partial
        send_rows(k, q1_send, q1_got, my_y * n_det + my_det, q1_ssem, q1_rsem, peers_xy)
        if not last:
            adjoint_start(r)
        new_norm = jnp.sum(add_rows(k, g2_got, g2_rsem), axis=1, keepdims=True)
        if k == 0:
            direction = gradient
            fd_ref[...] = fg_ref[...]
        else:
            beta = new_norm / norm
            direction = gradient + beta * direction
            fd_ref[...] = fg_ref[...] + beta * fd_ref[...]
        norm = new_norm
        q2_send[k] = add_rows(k, q1_got, q1_rsem)
        send_rows(k, q2_send, q2_got, slot_z, q2_ssem, q2_rsem, peers_z)
        if not last:
            applied = adjoint_wait(r) + damping * gradient
            swept = applied if k == 0 else applied + beta * swept
            forward(r + 1, swept)
        else:
            r_ref[...] = pick(sel, r_ref[...])
            fg_ref[...] = pick(sel, fd_ref[...])
        sums = jnp.sum(add_rows(k, q2_got, q2_rsem), axis=1, keepdims=True)
        curve = sums[0:1] if k == 0 else sums[0:1] + beta * (2.0 * sums[1:2] + beta * curve)
        step = norm / curve
        knots = step * direction if k == 0 else knots + step * direction
        if not last:
            gradient = gradient - step * swept
            norm_start(k + 1, gradient)
            r_ref[...] = r_ref[...] - step * fd_ref[...]
        else:
            r_out[...] = r_ref[...] - step * fg_ref[...]
    x_out[...] = knots[:params, :LANES]

    for r in range(ITERS + 1):
        wait_bytes(pred.at[r, pl.ds(0, tiles - per), :], a_send.at[r])
    for r in range(ITERS):
        wait_bytes(det_got.at[r, pl.ds(0, n_det - 1)], d_send.at[r])
        wait_bytes(prev_got.at[r], e_send.at[r])
        wait_bytes(next_got.at[r], e_send.at[r])
        for target, ssem in ((g1_got, g1_ssem), (g2_got, g2_ssem), (q1_got, q1_ssem), (q2_got, q2_ssem)):
            wait_bytes(target.at[r, pl.ds(0, target.shape[1] - 1)], ssem.at[r])


def local(n_track, n_det, jac, obs, match, tile_knot, tile_frac):
    tiles, params, width = jac.shape
    rounds = ITERS + 1
    n_y = TRACK_DIMS[0]
    dma = pltpu.SemaphoreType.DMA
    vmem = pl.BlockSpec(memory_space=pltpu.VMEM)
    row = (1, tiles)
    operands = (
        jnp.transpose(jac, (1, 0, 2)), obs,
        match.reshape(row), tile_knot.reshape(row), tile_frac.reshape(row),
    )
    return pl.pallas_call(
        functools.partial(kernel, n_track, n_det),
        out_shape=(
            jax.ShapeDtypeStruct((params, KNOT_DEV), F32),
            jax.ShapeDtypeStruct((tiles, width), F32),
        ),
        in_specs=[pl.BlockSpec(memory_space=pltpu.HBM)] * 5,
        out_specs=(vmem, vmem),
        scratch_shapes=[
            pltpu.VMEM((tiles, width), F32),
            pltpu.VMEM(row, jnp.int32),
            pltpu.VMEM(row, jnp.int32),
            pltpu.VMEM(row, F32),
            pltpu.VMEM((params, tiles, width), F32),
            pltpu.VMEM((params, width, tiles), F32),
            pltpu.VMEM((tiles, tiles), BF16),
            pltpu.VMEM((tiles, tiles), BF16),
            pltpu.VMEM((KNOT_DEV, tiles), BF16),
            pltpu.VMEM((8, tiles), F32),
            pltpu.VMEM((rounds, tiles, width), F32),
            pltpu.VMEM((rounds, tiles, width), F32),
            pltpu.VMEM((tiles, width), F32),
            pltpu.VMEM((tiles, width), F32),
            pltpu.VMEM((ROWS, tiles), F32),
            pltpu.VMEM((ROWS, tiles), F32),
            pltpu.VMEM((tiles, width), F32),
            pltpu.VMEM((ITERS, ROWS, KNOT_DEV), F32),
            pltpu.VMEM((ITERS, n_det, ROWS, KNOT_DEV), F32),
            pltpu.VMEM((ITERS, 2, 1, KNOT_DEV), F32),
            pltpu.VMEM((ITERS, n_det, 1, KNOT_DEV), F32),
            pltpu.VMEM((ITERS, n_det, 1, KNOT_DEV), F32),
            pltpu.VMEM((ITERS, 1, LANES), F32),
            pltpu.VMEM((ITERS, n_y, 1, LANES), F32),
            pltpu.VMEM((ITERS, 1, LANES), F32),
            pltpu.VMEM((ITERS, n_track // n_y, 1, LANES), F32),
            pltpu.VMEM((ITERS, 2, LANES), F32),
            pltpu.VMEM((ITERS, n_y * n_det, 2, LANES), F32),
            pltpu.VMEM((ITERS, 2, LANES), F32),
            pltpu.VMEM((ITERS, n_track // n_y, 2, LANES), F32),
            dma((4,)), dma, dma((rounds,)), dma((rounds, n_y)),
        ] + [dma((ITERS,))] * 13,
        compiler_params=pltpu.CompilerParams(
            collective_id=0, has_side_effects=True, vmem_limit_bytes=48 * 1024 * 1024
        ),
    )(*(pltpu.with_memory_space_constraint(value, pltpu.HBM) for value in operands))


def solution(mesh):
    in_specs = (P("track", None, "det"), P("track", "det"), P("track"), P("track"), P("track"))
    out_specs = (P(None, "track"), P("track", "det"))
    body = functools.partial(local, mesh.shape["track"], mesh.shape["det"])
    return jax.shard_map(body, mesh=mesh, in_specs=in_specs, out_specs=out_specs, check_vma=False)
```

time: 95.1 us -> 89.5 us (0.941)
  Pallas kernels: 91.3 us -> 87.5 us
  local copies, waits for them, and re-layouts: 2.96 us -> 1.3 us
    pallas_call x1, Pallas kernels: 91.3 us -> 87.5 us  [local(): pl.pallas_call(functools.partial(kernel, n_track, n_det), out_shape=(jax....]
    unnamed x2, local copies, waits for them, and re-layouts: 2.96 us -> 1.3 us
where the time goes in v3:
time: 89.5 us; the launch traced here: 89.4 us
  Pallas kernels  87.5 us (98%)
  local copies, waits for them, and re-layouts  1.3 us (1%)
    pallas_call x1, Pallas kernels, local(): pl.pallas_call(functools.partial(kernel, n_track, n_det), out_shape=(jax....  87.5 us

profile of v3, /device:TPU:1, one launch (start us, length us, event | category | flops | bytes accessed | tf_op | source)
XLA Modules:
  0.0 89.4 jit_solution(10991749695897781223)
XLA Ops:
  0.6 87.5 %shard_map.68 = (f32[12,128]{1,0:T(8,128)S(1)}, f32[512,128]{1,0:T(8,128)S(1)}) custom-call(f32[12,512,128]{2,1,0:T(8,128)} %bitcast.4, f32[512,128]{1,0:T(8,128)} %obs_hbm.1, s32[1,512]{1,0:T(1,128)} %bitcast.5, s32[1,512]{1,0:T(1,128)} %bitcast.6, f32[1,512]{1,0:T(1,128)} %bitcast.7), custom_call_target="tpu_custom_call" | custom-call | tf_op jit(solution)/shard_map/pallas_call | solution.py:381
  88.1 0.6 copy.9
  88.7 0.7 copy.10

commit v4 on v3

--- a/solution.py
+++ b/solution.py
@@ -225,7 +225,7 @@
         for p in range(params):
             spread_ref[p:p + 1, cols] = jnp.sum(jac_t[p, :, cols] * turned, axis=0, keepdims=True)
 
-    def adjoint_start(r):
+    def ends_start(r):
         sums = spread_ref[...]
         spill = to_row(jnp.sum(sums * weight[2:3], axis=1, keepdims=True))
         first_col = jnp.sum(sums * weight[3:4], axis=1, keepdims=True)
@@ -238,6 +238,10 @@
                     send_sem=e_send.at[r], recv_sem=rsem.at[r],
                     device_id=device, device_id_type=MESH,
                 ).start()
+        return spill, first_col
+
+    def sums_start(r, spill, first_col):
+        sums = spread_ref[...]
         parts = split3(sums * weight[0:1]) + split3(sums * weight[1:2])
         out = lax.dot_general(
             jnp.concatenate(parts, axis=0), hot[...], (((1,), (1,)), ((), ())), preferred_element_type=F32
@@ -255,25 +259,31 @@
                 device_id=device, device_id_type=MESH,
             ).start()
 
-    def adjoint_wait(r):
+    def sums_wait(r):
         wait_bytes(det_got.at[r, pl.ds(0, n_det - 1)], d_recv.at[r])
+        total = jnp.sum(det_got[r], axis=0)
+        beyond = jnp.where(me < n_track - 1, to_col(total[params:params + 1]), 0.0)
+        main = jnp.where(sub < params, total, 0.0)
+        return jnp.concatenate([main, jnp.where(lane == 0, beyond, 0.0)], axis=1)
+
+    def ends_wait(r):
         wait_bytes(prev_got.at[r], e_recv.at[r])
         wait_bytes(next_got.at[r], h_recv.at[r])
-        total = jnp.sum(det_got[r], axis=0)
         before = jnp.sum(prev_got[r], axis=0)
         after = jnp.sum(next_got[r], axis=0)
-        carried = jnp.where(me > 0, to_col(before), 0.0)
-        beyond = jnp.where(me < n_track - 1, to_col(total[params:params + 1] + after), 0.0)
-        main = jnp.where(sub < params, total, 0.0) + jnp.where(lane == 0, carried, 0.0)
-        return jnp.concatenate([main, jnp.where(lane == 0, beyond, 0.0)], axis=1)
-
-    def forward(r, field):
+        return jnp.where(me > 0, to_col(before), 0.0), jnp.where(me < n_track - 1, to_col(after), 0.0)
+
+    def forward(r, field, meanwhile=None):
         later = pltpu.roll(field, 2 * LANES - 1, 1)
         parts = split3(field[:, :LANES]) + split3(later[:, :LANES])
         out = jnp.dot(jnp.concatenate(parts, axis=0), hot[...], preferred_element_type=F32)
         low = (out[0:16] + out[16:32]) + out[32:48]
         high = (out[48:64] + out[64:80]) + out[80:96]
-        interp_ref[...] = low * weight[0:1] + high * weight[1:2]
+        interp = low * weight[0:1] + high * weight[1:2]
+        if meanwhile is not None:
+            meanwhile()
+        carried, beyond = ends_wait(r - 1)
+        interp_ref[...] = interp + carried * weight[3:4] + beyond * weight[2:3]
         for group in range(n_y):
             y = lax.rem(my_y + far_first_py(group, n_y), n_y)
             cols = pl.ds(pl.multiple_of(y * LANES, LANES), LANES)
@@ -282,14 +292,15 @@
                 total = total + jac_t[p, :, cols] * interp_ref[p:p + 1, cols]
             pred[r, cols, :] = jnp.transpose(total)
             exchange_start(r, group)
+        ends = [jnp.where(lane == 0, end, 0.0) for end in (carried, beyond)]
+        return field + jnp.concatenate(ends, axis=1)
 
     for rows in exchange_groups(0):
         misfit = pred[0, rows, :] - arrived[0, rows, :]
         r_ref[rows, :] = misfit
         adjoint_part(rows, misfit)
-    adjoint_start(0)
-    gradient = adjoint_wait(0)
-    forward(1, gradient)
+    sums_start(0, *ends_start(0))
+    gradient = forward(1, sums_wait(0))
 
     def norm_start(k, field):
         main = field[:, :LANES]
@@ -317,6 +328,8 @@
             own_part = own_part + 0.5 * jnp.sum(change * change, axis=0, keepdims=True)
             if not last:
                 adjoint_part(rows, change)
+        if not last:
+            ends = ends_start(r)
         main = gradient[:, :LANES]
         share = damping / n_det
         own_part = own_part + share * jnp.sum(main * main, axis=0, keepdims=True)
@@ -326,7 +339,7 @@
         q1_send[k] = partial
         send_rows(k, q1_send, q1_got, my_y * n_det + my_det, q1_ssem, q1_rsem, peers_xy)
         if not last:
-            adjoint_start(r)
+            sums_start(r, *ends)
         new_norm = jnp.sum(add_rows(k, g2_got, g2_rsem), axis=1, keepdims=True)
         if k == 0:
             direction = gradient
@@ -336,13 +349,16 @@
             direction = gradient + beta * direction
             fd_ref[...] = fg_ref[...] + beta * fd_ref[...]
         norm = new_norm
-        q2_send[k] = add_rows(k, q1_got, q1_rsem)
-        send_rows(k, q2_send, q2_got, slot_z, q2_ssem, q2_rsem, peers_z)
+
+        def pass_on():
+            q2_send[k] = add_rows(k, q1_got, q1_rsem)
+            send_rows(k, q2_send, q2_got, slot_z, q2_ssem, q2_rsem, peers_z)
+
         if not last:
-            applied = adjoint_wait(r) + damping * gradient
-            swept = applied if k == 0 else applied + beta * swept
-            forward(r + 1, swept)
+            applied = sums_wait(r) + damping * gradient
+            swept = forward(r + 1, applied if k == 0 else applied + beta * swept, pass_on)
         else:
+            pass_on()
             r_ref[...] = pick(sel, r_ref[...])
             fg_ref[...] = pick(sel, fd_ref[...])
         sums = jnp.sum(add_rows(k, q2_got, q2_rsem), axis=1, keepdims=True)
@@ -367,6 +383,17 @@
             wait_bytes(target.at[r, pl.ds(0, target.shape[1] - 1)], ssem.at[r])
 
 
+def put_out(knots, residual, x_out, r_out, sem):
+    copies = [
+        pltpu.make_async_copy(source, target, sem.at[i])
+        for i, (source, target) in enumerate(((residual, r_out), (knots, x_out)))
+    ]
+    for copy in copies:
+        copy.start()
+    for copy in copies:
+        copy.wait()
+
+
 def local(n_track, n_det, jac, obs, match, tile_knot, tile_frac):
     tiles, params, width = jac.shape
     rounds = ITERS + 1
@@ -378,7 +405,7 @@
         jnp.transpose(jac, (1, 0, 2)), obs,
         match.reshape(row), tile_knot.reshape(row), tile_frac.reshape(row),
     )
-    return pl.pallas_call(
+    knots, residual = pl.pallas_call(
         functools.partial(kernel, n_track, n_det),
         out_shape=(
             jax.ShapeDtypeStruct((params, KNOT_DEV), F32),
@@ -423,6 +450,18 @@
             collective_id=0, has_side_effects=True, vmem_limit_bytes=48 * 1024 * 1024
         ),
     )(*(pltpu.with_memory_space_constraint(value, pltpu.HBM) for value in operands))
+    hbm = pl.BlockSpec(memory_space=pltpu.HBM)
+    return pl.pallas_call(
+        put_out,
+        out_shape=(
+            jax.ShapeDtypeStruct((params, KNOT_DEV), F32),
+            jax.ShapeDtypeStruct((tiles, width), F32),
+        ),
+        in_specs=[vmem, vmem],
+        out_specs=(hbm, hbm),
+        scratch_shapes=[dma((2,))],
+        compiler_params=pltpu.CompilerParams(vmem_limit_bytes=2 * 1024 * 1024),
+    )(knots, residual)
 
 
 def solution(mesh):

time: 89.5 us -> 88.7 us (level)
  local copies, waits for them, and re-layouts: 1.3 us -> 0 us
    unnamed x2 -> x0, local copies, waits for them, and re-layouts: 1.3 us -> none
where the time goes in v4:
time: 88.7 us; the launch traced here: 88.6 us
  Pallas kernels  87.9 us (99%)
    pallas_call x1, Pallas kernels, local(): pl.pallas_call(functools.partial(kernel, n_track, n_det), out_shape=(jax....  87.2 us

profile of v4, /device:TPU:1, one launch (start us, length us, event | category | flops | bytes accessed | tf_op | source)
XLA Modules:
  0.0 88.6 jit_solution(5594527016093438125)
XLA Ops:
  0.6 87.2 %shard_map.68 = (f32[12,128]{1,0:T(8,128)S(1)}, f32[512,128]{1,0:T(8,128)S(1)}) custom-call(f32[12,512,128]{2,1,0:T(8,128)} %bitcast.4, f32[512,128]{1,0:T(8,128)} %obs_hbm.1, s32[1,512]{1,0:T(1,128)} %bitcast.5, s32[1,512]{1,0:T(1,128)} %bitcast.6, f32[1,512]{1,0:T(1,128)} %bitcast.7), custom_call_target="tpu_custom_call" | custom-call | tf_op jit(solution)/shard_map/pallas_call | solution.py:408
  87.8 0.7 shard_map.69
